TPU v7x, 32 devices: a whole 2x2x4 slice. The times are simulated.
32 devices in a mesh: groups: 2 (over x), ctx: 4 (over y, core), heads: 4 (over z).
Axes of the slice: x: 2, y: 2, z: 4, core: 2. Of those that a mesh axis runs over, the one named last changes fastest.
Arguments:
- tokens: bfloat16 [4096, 2048], P(('groups', 'ctx', 'heads')), parts along dimension 0, may hold values from -60 to 60
- state_in: float32 [4, 256, 128], P('heads', 'groups'), parts along dimension 1, may hold values from -256 to 256
- past_kv: bfloat16 [2, 1024, 512], P(None, 'groups', 'heads'), parts along dimension 1, may hold values from -6 to 6
- w_qkv: bfloat16 [2048, 3, 512], P(None, None, 'heads'), may hold values from -0.125 to 0.125
- w_out: bfloat16 [512, 2048], P('heads'), may hold values from -0.25 to 0.25
- w_gate: bfloat16 [16, 2048, 768], P(('ctx', 'heads')), may hold values from -0.125 to 0.125
- w_up: bfloat16 [16, 2048, 768], P(('ctx', 'heads')), may hold values from -0.125 to 0.125
- w_down: bfloat16 [16, 768, 2048], P(('ctx', 'heads')), may hold values from -0.21875 to 0.21875
- expert_ids: int32 [4096, 8], P(('groups', 'ctx', 'heads')), parts along dimension 0, may hold values from 0 to 15, all different within a row; in each aligned block of 128 rows (0 to 127, 128 to 255, ...) at most 128 rows name the same one
- gate_weights: float32 [4096, 8], P(('groups', 'ctx', 'heads')), parts along dimension 0, may hold values from 0.1 to 1
Outputs:
- mixed: bfloat16 [4096, 2048], P(('groups', 'ctx', 'heads')), parts along dimension 0
There are 2 independent parts, one for each index of `groups`. A program takes and returns all parts, laid end to end along the dimension named above; an argument that names none is the same for every part. Nothing has to cross between parts.
Inputs may be any that keep to these rules, and one draw needn't show every extreme that they name: `expert_ids`: each row names 8 different experts; in each aligned block of 128 rows (the rows of one device) no expert is named by more than 128 rows, a bound that some block reaches.
All inputs are finite; a program needn't handle non-finite values.
Results may differ from a plain program's by a relative error of at most 0.017.
Values may be sent and summed in bfloat16 or wider, within the bound.
A program may use at most 128 MiB of HBM per device.

v0:
```python
import math
import jax
import jax.numpy as jnp
from jax import lax
from jax.sharding import PartitionSpec as P

HDIM = 128
WINDOW = 512


def entering(x, axis, join, neutral):
    place = lax.axis_index(axis)
    gathered = lax.all_gather(x.astype(jnp.bfloat16), axis)
    state = jnp.zeros_like(x) + jnp.asarray(neutral, x.dtype)

    def one(lap, state):
        return join(state, lax.dynamic_index_in_dim(gathered, lap, 0, False).astype(x.dtype))

    return lax.fori_loop(0, place, one, state)


def from_behind(block, axis, distance):
    devices = range(lax.axis_size(axis))
    route = [(i - distance, i) for i in devices if i - distance in devices]
    return lax.ppermute(block, axis, route)


def normalize(value):
    return value * lax.rsqrt(jnp.mean(value * value, axis=-1, keepdims=True) + 1e-06)


def dense_experts(
    hidden_float, normed, w_gate, w_up, w_down, expert_ids, gate_weights, expert_count
):
    axes = ("ctx", "heads")
    exp_local = w_gate.shape[0]
    chosen = expert_ids[:, :, None] == jnp.arange(expert_count, dtype=jnp.int32)
    table = jnp.sum(jnp.where(chosen, gate_weights[:, :, None], 0.0), axis=1)
    weights = lax.all_gather(table, axes, axis=0, tiled=True)
    first = lax.axis_index(axes) * exp_local
    rows = lax.all_gather(normed, axes, axis=0, tiled=True)
    total = None
    for e in range(exp_local):
        gate_act = jnp.dot(rows, w_gate[e], preferred_element_type=jnp.float32)
        up_act = jnp.dot(rows, w_up[e], preferred_element_type=jnp.float32)
        hid = (jax.nn.silu(gate_act) * up_act).astype(jnp.bfloat16)
        out_rows = jnp.dot(hid, w_down[e], preferred_element_type=jnp.float32)
        weight = lax.dynamic_slice_in_dim(weights, first + e, 1, 1)
        part = weight * out_rows
        total = part if total is None else total + part
    routed = lax.psum_scatter(total.astype(jnp.bfloat16), axes, scatter_dimension=0, tiled=True)
    return (hidden_float + routed.astype(jnp.float32)).astype(jnp.bfloat16)


def on_device(
    tokens, state_in, past_kv, w_qkv, w_out, w_gate, w_up, w_down, expert_ids, gate_weights
):
    row_count, model_width = tokens.shape
    inner_width = w_qkv.shape[2]
    local_heads = inner_width // HDIM
    w_flat = w_qkv.reshape(model_width, 3 * inner_width)
    projected = jnp.dot(
        lax.all_gather(tokens, "heads", axis=0, tiled=True),
        w_flat,
        preferred_element_type=jnp.float32,
    ).astype(jnp.bfloat16)
    slab_rows = projected.shape[0]
    projected = projected.reshape(slab_rows, 3, local_heads, HDIM)
    query = jnp.transpose(projected[:, 0], (1, 0, 2))
    keys = jnp.transpose(projected[:, 1], (1, 0, 2))
    values = jnp.transpose(projected[:, 2], (1, 0, 2))
    local_state = jnp.einsum("hsd,hse->hde", keys, values, preferred_element_type=jnp.float32)
    earlier_state = entering(
        local_state, "ctx", lambda first, second: first + second, jnp.zeros_like(local_state)
    )
    start_state = state_in + earlier_state
    tail = jnp.stack([keys, values], axis=0)
    arrived = from_behind(tail, "ctx", 1)
    past = jnp.transpose(past_kv.reshape(2, WINDOW, local_heads, HDIM), (0, 2, 1, 3))
    previous = jnp.where(lax.axis_index("ctx") == 0, past, arrived)
    all_keys = jnp.concatenate([previous[0], keys], axis=1)
    all_values = jnp.concatenate([previous[1], values], axis=1)
    block_rows = min(slab_rows, 512)
    block_count = slab_rows // block_rows
    scale = 1.0 / math.sqrt(HDIM)
    causal = jnp.arange(block_rows)[:, None] >= jnp.arange(block_rows)[None, :]
    offsets = jnp.arange(WINDOW + block_rows)[None, :] - jnp.arange(block_rows)[:, None]
    in_window = (offsets > 0) & (offsets <= WINDOW)

    def block_step(state, index):
        first = index * block_rows
        carried = jnp.einsum(
            "hsd,hde->hse", query.astype(jnp.float32), state, precision=lax.Precision.HIGHEST
        )
        inside = jnp.einsum("hsd,htd->hst", query, keys, preferred_element_type=jnp.float32)
        inside = jnp.where(causal[None], inside, 0.0).astype(jnp.bfloat16)
        linear = carried + jnp.einsum(
            "hst,hte->hse", inside, values, preferred_element_type=jnp.float32
        )
        scores = (
            jnp.einsum("hsd,htd->hst", query, all_keys, preferred_element_type=jnp.float32) * scale
        )
        scores = jnp.where(in_window[None], scores, -jnp.inf)
        top_score = jnp.max(scores, axis=-1, keepdims=True)
        expo = jnp.exp(scores - top_score)
        probs = (expo / jnp.sum(expo, axis=-1, keepdims=True)).astype(jnp.bfloat16)
        window_out = jnp.einsum(
            "hst,hte->hse", probs, all_values, preferred_element_type=jnp.float32
        )
        combined = (normalize(linear) + window_out).astype(jnp.bfloat16)
        new_state = state + jnp.einsum(
            "hsd,hse->hde", keys, values, preferred_element_type=jnp.float32
        )
        return (new_state, combined)

    _, outs = lax.scan(block_step, start_state, jnp.arange(block_count, dtype=jnp.int32))
    heads_out = jnp.transpose(outs, (0, 2, 1, 3)).reshape(slab_rows, inner_width)
    regrouped = lax.all_to_all(heads_out, "heads", split_axis=0, concat_axis=1, tiled=True)
    attn = jnp.dot(
        regrouped,
        lax.all_gather(w_out, "heads", axis=0, tiled=True),
        preferred_element_type=jnp.float32,
    )
    hidden_state = (tokens.astype(jnp.float32) + attn).astype(jnp.bfloat16)
    hidden_float = hidden_state.astype(jnp.float32)
    normed = normalize(hidden_float).astype(jnp.bfloat16)
    ctx_count = lax.axis_size("ctx")
    head_count = lax.axis_size("heads")
    exp_local = w_gate.shape[0]
    expert_count = exp_local * ctx_count * head_count
    top_count = expert_ids.shape[1]
    capacity = max(2, 2 * row_count * top_count // expert_count)
    devices = ctx_count * head_count
    if row_count * devices <= expert_count * capacity:
        return dense_experts(
            hidden_float, normed, w_gate, w_up, w_down, expert_ids, gate_weights, expert_count
        )
    picks = expert_ids.reshape(-1)
    onehot = (picks[:, None] == jnp.arange(expert_count, dtype=jnp.int32)[None, :]).astype(
        jnp.int32
    )
    earlier = jnp.cumsum(onehot, axis=0) - onehot
    slots = jnp.sum(onehot * earlier, axis=1)
    destination = picks * capacity + slots
    source_rows = jnp.arange(row_count * top_count, dtype=jnp.int32) // top_count
    outgoing = jnp.zeros((expert_count * capacity, model_width), jnp.bfloat16)
    outgoing = outgoing.at[destination].set(normed[source_rows])
    sendable = outgoing.reshape(expert_count, 1, capacity, model_width)
    arrived_rows = lax.all_to_all(
        sendable, ("ctx", "heads"), split_axis=0, concat_axis=1, tiled=True
    )
    e_count, n_count, c_count, d_count = arrived_rows.shape
    flat = arrived_rows.reshape(e_count, n_count * c_count, d_count)
    gate_act = jnp.einsum("erd,edf->erf", flat, w_gate, preferred_element_type=jnp.float32)
    up_act = jnp.einsum("erd,edf->erf", flat, w_up, preferred_element_type=jnp.float32)
    hid = (jax.nn.silu(gate_act) * up_act).astype(jnp.bfloat16)
    out_rows = jnp.einsum("erf,efd->erd", hid, w_down, preferred_element_type=jnp.float32)
    finished = out_rows.astype(jnp.bfloat16).reshape(e_count, n_count, c_count, d_count)
    returned = lax.all_to_all(finished, ("ctx", "heads"), split_axis=1, concat_axis=0, tiled=True)
    returned = returned.reshape(expert_count * capacity, model_width)
    picked = returned[destination].reshape(row_count, top_count, model_width).astype(jnp.float32)
    routed = jnp.sum(gate_weights[:, :, None] * picked, axis=1)
    return (hidden_float + routed).astype(jnp.bfloat16)


def solution(mesh):
    return jax.shard_map(
        on_device,
        mesh=mesh,
        in_specs=(
            P(("groups", "ctx", "heads"), None),
            P("heads", "groups", None),
            P(None, "groups", "heads"),
            P(None, None, "heads"),
            P("heads", None),
            P(("ctx", "heads"), None, None),
            P(("ctx", "heads"), None, None),
            P(("ctx", "heads"), None, None),
            P(("groups", "ctx", "heads"), None),
            P(("groups", "ctx", "heads"), None),
        ),
        out_specs=P(("groups", "ctx", "heads"), None),
        check_vma=False,
    )
```

profile of v0, /device:TPU:0, one launch (start us, length us, event | category | flops | bytes accessed | tf_op | source)
XLA Modules:
  0.0 328.5 jit_solution(8045174008604358506)
XLA Ops:
  8.0 2.6 copy.27
  10.6 46.7 %all-gather.5.cloned.1.call-done = bf16[512,2048]{1,0:T(8,128)(2,1)} async-done(((bf16[128,2048]{1,0:T(8,128)(2,1)}), bf16[512,2048]{1,0:T(8,128)(2,1)}) %all-gather.5.cloned.1.call-update) | async-done | bytes 2097168 | tf_op jit(solution)/shard_map/all_gather | solution.py:63
  57.3 3.1 convolution_convert_fusion
  61.3 5.4 %all-gather = bf16[512,128]{1,0:T(8,128)(2,1)S(1)} all-gather(bf16[128,128]{1,0:T(8,128)(2,1)S(1)} %convolution_convert_fusion.1), channel_id=2, replica_groups=mesh['groups'=2,'ctx'=4,'heads'=4] {'ctx'}, dimensions={0}, use_global_device_ids=true | all-gather | bytes 163840 | tf_op jit(solution)/shard_map/all_gather | solution.py:13
  66.7 1.0 copy.35
  67.8 1.7 copy.34
  69.4 1.6 pad_maximum_fusion
  71.1 3.0 collective-permute-start
  74.0 2.0 fusion.26
  76.0 2.3 multiply_reduce_fusion.1
  78.3 1.1 bitcast_select_fusion
  79.4 1.5 fusion.39
  82.1 0.8 copy.33
  82.8 3.5 %all-to-all-start = ((bf16[4,128,128]{1,2,0:T(8,128)(2,1)}), bf16[4,128,128]{1,2,0:T(8,128)(2,1)S(1)}, u32[]{:S(2)}, u32[]{:S(2)}) async-start(bf16[4,128,128]{1,2,0:T(8,128)(2,1)} %copy.33), calls=%async_computation | async-start | bytes 262144 | tf_op jit(solution)/shard_map/all_to_all | solution.py:118
  86.3 19.8 %all-gather.7.cloned.1.call-done = bf16[512,2048]{1,0:T(8,128)(2,1)} async-done(((bf16[128,2048]{1,0:T(8,128)(2,1)}), bf16[512,2048]{1,0:T(8,128)(2,1)}) %all-gather.7.cloned.1.call-update) | async-done | bytes 2097168 | tf_op jit(solution)/shard_map/all_gather | solution.py:121
  106.2 2.2 multiply_reduce_fusion
  108.4 1.0 copy-done.1
  109.4 0.9 multiply_convert_fusion.2
  110.5 33.1 %all_gather.22 = f32[2048,16]{0,1:T(8,128)S(1)} all-gather(f32[128,16]{0,1:T(8,128)S(1)} %select_reduce_fusion), channel_id=1, replica_groups=mesh['groups'=2,'ctx'=4,'heads'=4] {'ctx','heads'}, dimensions={0}, use_global_device_ids=true | all-gather | bytes 139264 | tf_op jit(solution)/shard_map/all_gather | solution.py:39
  143.6 41.7 %all-gather.9.cloned.1.call-done = bf16[2048,2048]{1,0:T(8,128)(2,1)} async-done(((bf16[128,2048]{1,0:T(8,128)(2,1)}), bf16[2048,2048]{1,0:T(8,128)(2,1)}) %all-gather.9.cloned.1.call-update) | async-done | bytes 8388624 | tf_op jit(solution)/shard_map/all_gather | solution.py:41
  185.3 11.7 %fusion.3 = f32[2048,768]{1,0:T(8,128)} fusion(bf16[2048,2048]{1,0:T(8,128)(2,1)} %all-gather.9.cloned.1.call-done, bf16[1,2048,768]{2,1,0:T(8,128)(2,1)} %param.17), kind=kOutput, calls=%fused_computation.5 | convolution fusion | flops 6442450944 | bytes 17825792 | tf_op jit(solution)/shard_map/dot_general | solution.py:44
  197.0 20.6 %multiply_convert_fusion = bf16[2048,2048]{1,0:T(8,128)(2,1)} fusion(f32[2048]{0:T(1024)S(1)} %bitcast.98, f32[2048,768]{1,0:T(8,128)} %fusion.3, bf16[2048,2048]{1,0:T(8,128)(2,1)} %all-gather.9.cloned.1.call-done, bf16[1,768,2048]{2,1,0:T(8,128)(2,1)S(1)} %copy-done, bf16[1,2048,768]{2,1,0:T(8,128)(2,1)} %param.18), kind=kOutput, calls=%fused_computation.1 | convolution fusion | flops 12902727680 | bytes 29368320 | tf_op jit(solution)/shard_map/dot_general | solution.py:47
  217.6 102.2 %reduce-scatter.2.cloned.1.call-done = bf16[128,2048]{1,0:T(8,128)(2,1)} async-done(((bf16[2048,2048]{1,0:T(8,128)(2,1)}), bf16[128,2048]{1,0:T(8,128)(2,1)}) %reduce-scatter.2.cloned.1.call-update) | async-done | bytes 524304 | tf_op jit(solution)/shard_map/reduce_scatter | solution.py:51
  319.7 2.3 add_convert_fusion
  (37 shorter events, 3.7 us)
Async XLA Ops:
  6.5 190.4 %copy-start = (bf16[1,768,2048]{2,1,0:T(8,128)(2,1)S(1)}, bf16[1,768,2048]{2,1,0:T(8,128)(2,1)}, u32[]{:S(2)}) copy-start(bf16[1,768,2048]{2,1,0:T(8,128)(2,1)} %param.19) | copy-start | bytes 9437188
  6.5 50.8 %all-gather.5.cloned.1.call-start = ((), (), s32[]{:S(2)}) async-start(), calls=%async_computation.2 | async-start | bytes 2621440 | tf_op jit(solution)/shard_map/all_gather | solution.py:63
  7.3 98.9 %all-gather.7.cloned.1.call-start = ((), (), s32[]{:S(2)}) async-start(), calls=%async_computation.3 | async-start | bytes 2621440 | tf_op jit(solution)/shard_map/all_gather | solution.py:121
  57.3 16.7 %copy-start.4 = (f32[1,128,128]{2,1,0:T(8,128)S(1)}, f32[1,128,128]{2,1,0:T(8,128)}, u32[]{:S(2)}) copy-start(f32[1,128,128]{2,1,0:T(8,128)} %param.13) | copy-start | bytes 196612
  60.4 6.3 %copy-start.3 = (bf16[512,384]{0,1:T(8,128)(2,1)}, bf16[512,384]{0,1:T(8,128)(2,1)S(1)}, u32[]{:S(2)}) copy-start(bf16[512,384]{0,1:T(8,128)(2,1)S(1)} %convolution_convert_fusion) | copy-start | bytes 1179652
  71.1 7.3 %collective-permute-start = (bf16[2,1,512,128]{3,2,1,0:T(8,128)(2,1)}, bf16[2,1,512,128]{3,2,1,0:T(8,128)(2,1)}, u32[]{:S(2)}, u32[]{:S(2)}) collective-permute-start(bf16[2,1,512,128]{3,2,1,0:T(8,128)(2,1)} %pad_maximum_fusion), channel_id=1, source_target_pairs={{0,4},{4,8},{8,12},{1,5},{5,9},{9,13},{2,6},{6,10},{10,14},{3,7},{... | collective-permute-start | bytes 786440 | tf_op jit(solution)/shard_map/ppermute | solution.py:25
  74.0 5.4 %copy-start.2 = (bf16[512,1,1,128]{3,0,2,1:T(8,128)(2,1)S(1)}, bf16[512,1,1,128]{3,0,2,1:T(8,128)(2,1)}, u32[]{:S(2)}) copy-start(bf16[512,1,1,128]{3,0,2,1:T(8,128)(2,1)} %copy.34) | copy-start | bytes 393220
  79.4 2.1 copy-start.7
  82.8 27.6 %copy-start.5 = (f32[128,8]{0,1:T(8,128)S(1)}, f32[128,8]{0,1:T(8,128)}, u32[]{:S(2)}) copy-start(f32[128,8]{0,1:T(8,128)} %param.21) | copy-start | bytes 12292
  82.8 27.6 %copy-start.6 = (s32[128,8]{0,1:T(8,128)S(1)}, s32[128,8]{0,1:T(8,128)}, u32[]{:S(2)}) copy-start(s32[128,8]{0,1:T(8,128)} %param.20) | copy-start | bytes 12292
  82.8 23.4 %all-to-all-start = ((bf16[4,128,128]{1,2,0:T(8,128)(2,1)}), bf16[4,128,128]{1,2,0:T(8,128)(2,1)S(1)}, u32[]{:S(2)}, u32[]{:S(2)}) async-start(bf16[4,128,128]{1,2,0:T(8,128)(2,1)} %copy.33), calls=%async_computation | async-start | bytes 262144 | tf_op jit(solution)/shard_map/all_to_all | solution.py:118
  86.3 99.0 %all-gather.9.cloned.1.call-start = ((), (), s32[]{:S(2)}) async-start(), calls=%async_computation.4 | async-start | bytes 8912896 | tf_op jit(solution)/shard_map/all_gather | solution.py:41
  108.4 1.0 copy-start.1
  110.4 209.4 %reduce-scatter.2.cloned.1.call-start = ((), (), s32[]{:S(2)}) async-start(), calls=%async_computation.5 | async-start | bytes 8912896 | tf_op jit(solution)/shard_map/reduce_scatter | solution.py:51
Sparse Core Ops, SparseCore 0:
  8.9 48.3 all-gather.4
  58.9 47.2 all-gather.6
  110.5 74.7 all-gather.8
  217.7 101.9 reduce-scatter.1
where the time goes:
time: 329 us
  waiting for transfers between devices  212 us (64%)
  matrix products  44.1 us (13%)
  blocking collectives  38.5 us (12%)
  between operations  13.3 us (4%)
  local copies, waits for them, and re-layouts  7.86 us (2%)
  starting transfers between devices  6.54 us (2%)
  other arithmetic  6.41 us (2%)
    reduce_scatter x1, waiting for transfers between devices, dense_experts(): lax.psum_scatter(total.astype(jnp.bfloat16), axes, scatter_dimension=0, t...  102 us
    all_gather x1, waiting for transfers between devices, on_device(): lax.all_gather(tokens, 'heads', axis=0, tiled=True)  46.7 us
    all_gather x1, waiting for transfers between devices, dense_experts(): rows = lax.all_gather(normed, axes, axis=0, tiled=True)  41.7 us
    all_gather x1, blocking collectives, dense_experts(): weights = lax.all_gather(table, axes, axis=0, tiled=True)  33.1 us
    dot_general x1, matrix products, dense_experts(): out_rows = jnp.dot(hid, w_down[e], preferred_element_type=jnp.float32)  20.6 us
    all_gather x1, waiting for transfers between devices, on_device(): lax.all_gather(w_out, 'heads', axis=0, tiled=True)  19.8 us
    dot_general x1, matrix products, dense_experts(): gate_act = jnp.dot(rows, w_gate[e], preferred_element_type=jnp.float32)  11.7 us
  transfers between devices with their start and end apart: 6, of which 4 were waited for; matrix products, arithmetic and copies ran while one was open for 6% of the time, Pallas kernels for 0%

commit v1 on v0

--- a/solution.py
+++ b/solution.py
@@ -36,9 +36,17 @@
     exp_local = w_gate.shape[0]
     chosen = expert_ids[:, :, None] == jnp.arange(expert_count, dtype=jnp.int32)
     table = jnp.sum(jnp.where(chosen, gate_weights[:, :, None], 0.0), axis=1)
-    weights = lax.all_gather(table, axes, axis=0, tiled=True)
     first = lax.axis_index(axes) * exp_local
-    rows = lax.all_gather(normed, axes, axis=0, tiled=True)
+
+    def write_islands(payload, xin, along_axis):
+        mat_out = jnp.split(
+            lax.all_gather(jnp.concatenate([payload, xin], 1), along_axis, axis=0, tiled=True),
+            [payload.shape[1]],
+            1,
+        )
+        return mat_out
+
+    weights, rows = write_islands(table, normed, axes)
     total = None
     for e in range(exp_local):
         gate_act = jnp.dot(rows, w_gate[e], preferred_element_type=jnp.float32)

time: 329 us -> 359 us (1.091)
  waiting for transfers between devices: 212 us -> 269 us
  blocking collectives: 38.5 us -> 5.4 us
    all_gather x1, waiting for transfers between devices: 41.7 us -> 97.5 us  [write_islands(): lax.all_gather(jnp.concatenate([payload, xin], 1), along_axis, axis=0, ti...]
    all_gather x1 -> x0, blocking collectives: 33.1 us -> none  [dense_experts(): weights = lax.all_gather(table, axes, axis=0, tiled=True)]
where the time goes in v1:
time: 359 us; the launch traced here: 358 us
  waiting for transfers between devices  269 us (75%)
  matrix products  46.8 us (13%)
  between operations  13.3 us (4%)
  local copies, waits for them, and re-layouts  10.2 us (3%)
  other arithmetic  7.02 us (2%)
  starting transfers between devices  6.58 us (2%)
  blocking collectives  5.4 us (2%)
    reduce_scatter x1, waiting for transfers between devices, dense_experts(): lax.psum_scatter(total.astype(jnp.bfloat16), axes, scatter_dimension=0, t...  104 us
    all_gather x1, waiting for transfers between devices, write_islands(): lax.all_gather(jnp.concatenate([payload, xin], 1), along_axis, axis=0, ti...  97.5 us
    all_gather x1, waiting for transfers between devices, on_device(): lax.all_gather(tokens, 'heads', axis=0, tiled=True)  46.7 us
    dot_general x1, matrix products, dense_experts(): out_rows = jnp.dot(hid, w_down[e], preferred_element_type=jnp.float32)  22.7 us
    all_gather x1, waiting for transfers between devices, on_device(): lax.all_gather(w_out, 'heads', axis=0, tiled=True)  19.8 us
    dot_general x1, matrix products, dense_experts(): gate_act = jnp.dot(rows, w_gate[e], preferred_element_type=jnp.float32)  12.2 us
  transfers between devices with their start and end apart: 6, of which 4 were waited for; matrix products, arithmetic and copies ran while one was open for 6% of the time, Pallas kernels for 0%

profile of v1, /device:TPU:0, one launch (start us, length us, event | category | flops | bytes accessed | tf_op | source)
XLA Modules:
  0.0 358.2 jit_solution(7078707776119002102)
XLA Ops:
  8.0 2.6 copy.27
  10.6 46.7 %all-gather.5.cloned.1.call-done = bf16[512,2048]{1,0:T(8,128)(2,1)} async-done(((bf16[128,2048]{1,0:T(8,128)(2,1)}), bf16[512,2048]{1,0:T(8,128)(2,1)}) %all-gather.5.cloned.1.call-update) | async-done | bytes 2097168 | tf_op jit(solution)/shard_map/all_gather | solution.py:71
  57.3 3.1 convolution_convert_fusion
  61.3 5.4 %all-gather = bf16[512,128]{1,0:T(8,128)(2,1)S(1)} all-gather(bf16[128,128]{1,0:T(8,128)(2,1)S(1)} %convolution_convert_fusion.1), channel_id=2, replica_groups=mesh['groups'=2,'ctx'=4,'heads'=4] {'ctx'}, dimensions={0}, use_global_device_ids=true | all-gather | bytes 163840 | tf_op jit(solution)/shard_map/all_gather | solution.py:13
  66.7 1.0 copy.36
  67.8 1.7 copy.35
  69.4 1.6 pad_maximum_fusion.1
  71.1 2.9 collective-permute-start
  74.0 2.0 fusion.34
  76.0 2.3 multiply_reduce_fusion.1
  78.3 1.1 bitcast_select_fusion
  79.4 1.5 fusion.47
  82.1 0.8 copy.33
  82.9 3.3 all-to-all-start
  86.4 19.8 %all-gather.7.cloned.1.call-done = bf16[512,2048]{1,0:T(8,128)(2,1)} async-done(((bf16[128,2048]{1,0:T(8,128)(2,1)}), bf16[512,2048]{1,0:T(8,128)(2,1)}) %all-gather.7.cloned.1.call-update) | async-done | bytes 2097168 | tf_op jit(solution)/shard_map/all_gather | solution.py:129
  106.2 2.2 multiply_reduce_fusion
  108.4 1.0 copy-done.1
  109.5 1.4 pad_maximum_fusion
  111.2 97.5 %all-gather.9.cloned.1.call-done = f32[2048,2064]{1,0:T(8,128)} async-done(((f32[128,2064]{1,0:T(8,128)}), f32[2048,2064]{1,0:T(8,128)}) %all-gather.9.cloned.1.call-update) | async-done | bytes 16908304 | tf_op jit(solution)/shard_map/all_gather | solution.py:43
  208.7 1.4 split.8
  210.9 12.2 %fusion.2 = f32[2048,768]{1,0:T(8,128)} fusion(f32[2048,2064]{1,0:T(8,128)} %all-gather.9.cloned.1.call-done, bf16[1,2048,768]{2,1,0:T(8,128)(2,1)S(1)} %copy-done.7), kind=kOutput, calls=%fused_computation.4 | convolution fusion | flops 6442450944 | bytes 17825792 | tf_op jit(solution)/shard_map/dot_general | solution.py:52
  223.1 22.7 %multiply_convert_fusion = bf16[2048,2048]{1,0:T(8,128)(2,1)} fusion(f32[2048]{0:T(1024)S(1)} %dynamic-slice_reduce_fusion, f32[2048,768]{1,0:T(8,128)} %fusion.2, f32[2048,2064]{1,0:T(8,128)} %all-gather.9.cloned.1.call-done, bf16[1,768,2048]{2,1,0:T(8,128)(2,1)S(1)} %copy-done, bf16[1,2048,768]{2,1,0:T(8,128)(2,1)} %param.18), kind=kOutput, calls=%fused_computation.1 | convolution fusion | flops 12902727680 | bytes 29368320 | tf_op jit(solution)/shard_map/dot_general | solution.py:55
  245.8 103.6 %reduce-scatter.2.cloned.1.call-done = bf16[128,2048]{1,0:T(8,128)(2,1)} async-done(((bf16[2048,2048]{1,0:T(8,128)(2,1)}), bf16[128,2048]{1,0:T(8,128)(2,1)}) %reduce-scatter.2.cloned.1.call-update) | async-done | bytes 524304 | tf_op jit(solution)/shard_map/reduce_scatter | solution.py:59
  349.4 2.3 add_convert_fusion
  (41 shorter events, 4.8 us)
Async XLA Ops:
  6.5 216.6 %copy-start = (bf16[1,768,2048]{2,1,0:T(8,128)(2,1)S(1)}, bf16[1,768,2048]{2,1,0:T(8,128)(2,1)}, u32[]{:S(2)}) copy-start(bf16[1,768,2048]{2,1,0:T(8,128)(2,1)} %param.19) | copy-start | bytes 9437188
  6.5 50.8 %all-gather.5.cloned.1.call-start = ((), (), s32[]{:S(2)}) async-start(), calls=%async_computation.2 | async-start | bytes 2621440 | tf_op jit(solution)/shard_map/all_gather | solution.py:71
  7.3 98.9 %all-gather.7.cloned.1.call-start = ((), (), s32[]{:S(2)}) async-start(), calls=%async_computation.3 | async-start | bytes 2621440 | tf_op jit(solution)/shard_map/all_gather | solution.py:129
  57.3 16.7 %copy-start.4 = (f32[1,128,128]{2,1,0:T(8,128)S(1)}, f32[1,128,128]{2,1,0:T(8,128)}, u32[]{:S(2)}) copy-start(f32[1,128,128]{2,1,0:T(8,128)} %param.13) | copy-start | bytes 196612
  60.4 6.3 %copy-start.3 = (bf16[512,384]{0,1:T(8,128)(2,1)}, bf16[512,384]{0,1:T(8,128)(2,1)S(1)}, u32[]{:S(2)}) copy-start(bf16[512,384]{0,1:T(8,128)(2,1)S(1)} %convolution_convert_fusion) | copy-start | bytes 1179652
  71.1 7.3 %collective-permute-start = (bf16[2,1,512,128]{3,2,1,0:T(8,128)(2,1)}, bf16[2,1,512,128]{3,2,1,0:T(8,128)(2,1)}, u32[]{:S(2)}, u32[]{:S(2)}) collective-permute-start(bf16[2,1,512,128]{3,2,1,0:T(8,128)(2,1)} %pad_maximum_fusion.1), channel_id=1, source_target_pairs={{0,4},{4,8},{8,12},{1,5},{5,9},{9,13},{2,6},{6,10},{10,14},{3,7},{... | collective-permute-start | bytes 786440 | tf_op jit(solution)/shard_map/ppermute | solution.py:25
  74.0 5.4 %copy-start.2 = (bf16[512,1,1,128]{3,0,2,1:T(8,128)(2,1)S(1)}, bf16[512,1,1,128]{3,0,2,1:T(8,128)(2,1)}, u32[]{:S(2)}) copy-start(bf16[512,1,1,128]{3,0,2,1:T(8,128)(2,1)} %copy.35) | copy-start | bytes 393220
  79.4 2.1 copy-start.8
  81.5 4.8 %copy-start.5 = (f32[128,8]{0,1:T(8,128)S(1)}, f32[128,8]{0,1:T(8,128)}, u32[]{:S(2)}) copy-start(f32[128,8]{0,1:T(8,128)} %param.21) | copy-start | bytes 12292
  81.5 4.8 %copy-start.6 = (s32[128,8]{0,1:T(8,128)S(1)}, s32[128,8]{0,1:T(8,128)}, u32[]{:S(2)}) copy-start(s32[128,8]{0,1:T(8,128)} %param.20) | copy-start | bytes 12292
  82.9 23.3 %all-to-all-start = ((bf16[4,128,128]{1,2,0:T(8,128)(2,1)}), bf16[4,128,128]{1,2,0:T(8,128)(2,1)S(1)}, u32[]{:S(2)}, u32[]{:S(2)}) async-start(bf16[4,128,128]{1,2,0:T(8,128)(2,1)} %copy.33), calls=%async_computation | async-start | bytes 262144 | tf_op jit(solution)/shard_map/all_to_all | solution.py:126
  86.2 122.4 %all-gather.9.cloned.1.call-start = ((), (), s32[]{:S(2)}) async-start(), calls=%async_computation.4 | async-start | bytes 18939904 | tf_op jit(solution)/shard_map/all_gather | solution.py:43
  108.4 1.0 copy-start.1
  111.0 238.5 %reduce-scatter.2.cloned.1.call-start = ((), (), s32[]{:S(2)}) async-start(), calls=%async_computation.5 | async-start | bytes 8912896 | tf_op jit(solution)/shard_map/reduce_scatter | solution.py:59
  208.7 2.2 copy-start.7
Sparse Core Ops, SparseCore 0:
  8.9 48.3 all-gather.4
  58.9 47.2 all-gather.6
  111.1 97.5 all-gather.8
  245.9 103.4 reduce-scatter.1
